TPU v7x, 32 devices: a whole 2x2x4 slice. The times are simulated.
32 devices in a mesh: dp: 8 (over y, x, core), exch: 4 (over z).
Axes of the slice: x: 2, y: 2, z: 4, core: 2. Of those that a mesh axis runs over, the one named last changes fastest.
Arguments:
- x_raw: bfloat16 [1024, 2048], P('exch', 'dp'), may hold values from -6 to 6
- bc_raw: bfloat16 [1024, 256], P(('exch', 'dp')), may hold values from -6 to 6
- dt_raw: bfloat16 [32, 1024], P('dp', 'exch'), may hold values from -4 to 4
- cotangent: bfloat16 [1024, 2048], P('exch', 'dp'), may hold values from -6 to 6
- ssm_state: bfloat16 [8, 32, 64, 128], P('exch', 'dp'), may hold values from -0.625 to 0.625
- conv_x_state: bfloat16 [8, 3, 2048], P('exch', None, 'dp'), may hold values from -6 to 6
- conv_bc_state: bfloat16 [8, 3, 256], P('exch'), may hold values from -6 to 6
- owner: int32 [8], P('exch'), may hold values from 0 to 3, as said below
- resp_len: int32 [8], P('exch'), may hold values from 32 to 128, as said below
- conv_x_weight: float32 [4, 2048], P(None, 'dp'), may hold values from -3 to 3
- conv_bc_weight: float32 [4, 256], replicated, may hold values from -3 to 3
- dt_bias: float32 [32], P('dp'), may hold values from -5 to -3
- a_log: float32 [32], P('dp'), may hold values from -2.3 to 2.1
- skip_d: float32 [32], P('dp'), may hold values from 0.5 to 1.5
Outputs:
- grad_x: bfloat16 [1024, 2048], P('exch', 'dp')
- grad_bc: bfloat16 [1024, 256], P(('exch', 'dp'))
- grad_dt: bfloat16 [32, 1024], P('dp', 'exch')
- grad_conv_x: float32 [4, 2048], P(None, 'dp')
- grad_conv_bc: float32 [4, 256], replicated
- grad_heads: float32 [3, 32], P(None, 'dp')
Inputs may be any that keep to these rules, and one draw needn't show every extreme that they name: `owner`: among the 2 prompts of one holder (an aligned block along exch) no learner index occurs more than 1 times, and some learner index occurs exactly 1 times; over all 8 prompts every learner index occurs exactly 2 times. `resp_len`: every learner's block of 2 responses holds a response of length 128.
All inputs are finite; a program needn't handle non-finite values.
Results may differ from a plain program's by a relative error of at most 0.001.
Values may be sent and summed in bfloat16 or wider, within the bound.
A program may use at most 64 MiB of HBM per device.

v0:
```python
import jax
import jax.numpy as jnp
from jax import lax
from jax.sharding import PartitionSpec as P

DEV_GROUP = 8
SPAN = 128
GROUP = 1
CAP = 1


PRECISE = lax.Precision.HIGHEST


def conv_pre(raw, state, weight):
    padded = jnp.concatenate([state, raw], axis=1)
    length = raw.shape[1]
    total = padded[:, 0:length] * weight[0]
    for offset in range(1, weight.shape[0]):
        total = total + padded[:, offset : offset + length] * weight[offset]
    return total


def ssd_output(values, proj_b, proj_c, steps, rate, skip, start, block):
    rows, length, heads, width = values.shape
    count = length // block
    value_blocks = values.reshape(rows, count, block, heads, width)
    b_blocks = proj_b.reshape(rows, count, block, proj_b.shape[-1])
    c_blocks = proj_c.reshape(rows, count, block, proj_c.shape[-1])
    step_blocks = steps.reshape(rows, count, block, heads)
    logs = jnp.cumsum(-rate * step_blocks, axis=2)
    causal = jnp.tril(jnp.ones((block, block), jnp.float32))
    spread = logs[:, :, :, None, :] - logs[:, :, None, :, :]
    decays = jnp.exp(jnp.where(causal[:, :, None] > 0.5, spread, 0.0)) * causal[:, :, None]
    scores = jnp.einsum("rntk,rnsk->rnts", c_blocks, b_blocks, precision=PRECISE)
    weighted = value_blocks * step_blocks[..., None]
    mixing = scores[..., None] * decays
    intra = jnp.einsum("rntsh,rnshp->rnthp", mixing, weighted, precision=PRECISE)
    entry = jnp.exp(logs[:, 0])
    carried = jnp.einsum("rtk,rhpk->rthp", c_blocks[:, 0], start, precision=PRECISE)
    pieces = [carried * entry[..., None]]
    inter = jnp.stack(pieces, axis=1)
    output = intra + inter + skip[:, None] * value_blocks
    return output.reshape(rows, length, heads, width)


def window_loss(
    x_rows,
    bc_act,
    dt_rows,
    x_weight,
    bias,
    decay_log,
    skip,
    x_prev,
    start,
    cotan,
    mask,
    heads,
    block,
):
    x_act = jax.nn.silu(conv_pre(x_rows, x_prev, x_weight))
    rows, length, channels = x_rows.shape
    values = x_act.reshape(rows, length, heads, channels // heads)
    half = bc_act.shape[-1] // 2
    steps = jax.nn.softplus(dt_rows + bias)
    output = ssd_output(
        values,
        bc_act[..., :half],
        bc_act[..., half:],
        steps,
        jnp.exp(decay_log),
        skip,
        start,
        block,
    )
    return jnp.sum(output.reshape(rows, length, channels) * cotan * mask[..., None])


def local(
    x_raw,
    bc_raw,
    dt_raw,
    cotangent,
    ssm_state,
    conv_x_state,
    conv_bc_state,
    owner,
    resp_len,
    conv_x_weight,
    conv_bc_weight,
    dt_bias,
    a_log,
    skip_d,
):
    peer_count = lax.axis_size("exch")
    slices = lax.axis_size("dp")
    prompts = owner.shape[0]
    responses = resp_len.shape[0]
    head_count = dt_raw.shape[0]
    tokens = x_raw.shape[0]
    channels = x_raw.shape[1]
    pair_width = 2 * ssm_state.shape[-1]
    conv_depth = conv_x_state.shape[1]
    length = tokens // responses
    row_count = bc_raw.shape[0]
    groups = bc_raw.shape[1] // pair_width
    my_group = lax.axis_index("dp") // DEV_GROUP
    targets = jnp.arange(peer_count, dtype=jnp.int32)
    match = (owner[:, None] == targets[None, :]).astype(jnp.int32)
    earlier = jnp.cumsum(match, axis=0) - match
    places = jnp.sum(earlier * match, axis=1)
    slot_ids = jnp.arange(CAP, dtype=jnp.int32)
    routing = (match[:, :, None] == 1) & (places[:, None, None] == slot_ids[None, None, :])
    routing = routing.reshape(prompts, peer_count * CAP).astype(jnp.bfloat16)

    def pack_slots(values):
        moved = jnp.dot(routing.T, values.reshape(prompts, -1), preferred_element_type=jnp.float32)
        return moved.astype(jnp.bfloat16).reshape(peer_count, CAP, -1)

    bc_state = lax.dynamic_slice_in_dim(conv_bc_state, my_group * pair_width, pair_width, 2)
    filled = jnp.sum(routing, axis=0).reshape(peer_count, CAP)
    got_ssm, got_x, got_bc, got_fill = (
        lax.all_to_all(pack_slots(ssm_state), "exch", split_axis=0, concat_axis=0, tiled=True),
        lax.all_to_all(pack_slots(conv_x_state), "exch", split_axis=0, concat_axis=0, tiled=True),
        lax.all_to_all(pack_slots(bc_state), "exch", split_axis=0, concat_axis=0, tiled=True),
        lax.all_to_all(filled, "exch", split_axis=0, concat_axis=0, tiled=True),
    )
    present = (got_fill.reshape(peer_count * CAP) > 0.5).astype(jnp.int32)
    position = jnp.cumsum(present) - 1
    owned_ids = jnp.arange(prompts, dtype=jnp.int32)
    select = ((present[None, :] == 1) & (position[None, :] == owned_ids[:, None])).astype(
        jnp.bfloat16
    )

    def unpack(values, shape):
        chosen = jnp.dot(
            select, values.reshape(peer_count * CAP, -1), preferred_element_type=jnp.float32
        )
        return jnp.repeat(chosen, GROUP, axis=0).reshape(shape)

    start_state = unpack(got_ssm, (responses, head_count, channels // head_count, -1))
    x_prev = unpack(got_x, (responses, conv_depth, channels))
    bc_prev = unpack(got_bc, (responses, conv_depth, pair_width))
    gathered = lax.all_gather(bc_raw, "dp", axis=0, tiled=True)
    bc_local = lax.dynamic_slice_in_dim(gathered, my_group * pair_width, pair_width, 1)
    x_rows = x_raw.astype(jnp.float32).reshape(responses, length, channels)
    bc_rows = bc_local.astype(jnp.float32).reshape(responses, length, pair_width)
    cot_rows = cotangent.astype(jnp.float32).reshape(responses, length, channels)
    dt_rows = dt_raw.astype(jnp.float32).T.reshape(responses, length, head_count)
    live_mask = (jnp.arange(length, dtype=jnp.int32)[None, :] < resp_len[:, None]).astype(
        jnp.float32
    )
    bc_weight = lax.dynamic_slice_in_dim(conv_bc_weight, my_group * pair_width, pair_width, 1)
    bc_pre = conv_pre(bc_rows, bc_prev, bc_weight)
    bc_act, silu_back = jax.vjp(jax.nn.silu, bc_pre)

    def local_loss(x_in, bc_in, dt_in, x_weight, bias, decay_log, skip):
        return window_loss(
            x_in,
            bc_in,
            dt_in,
            x_weight,
            bias,
            decay_log,
            skip,
            x_prev,
            start_state,
            cot_rows,
            live_mask,
            head_count,
            SPAN,
        )

    grad_xr, grad_bca, grad_dtr, grad_wx, grad_bias, grad_decay, grad_skip = jax.grad(
        local_loss, argnums=(0, 1, 2, 3, 4, 5, 6)
    )(x_rows, bc_act, dt_rows, conv_x_weight, dt_bias, a_log, skip_d)
    grad_pre = silu_back(grad_bca)[0]
    unused, conv_back = jax.vjp(
        lambda raw, weight: conv_pre(raw, bc_prev, weight), bc_rows, bc_weight
    )
    grad_raw, grad_wbc = conv_back(grad_pre)
    returned = lax.all_to_all(
        grad_raw.reshape(slices, row_count, pair_width),
        "dp",
        split_axis=0,
        concat_axis=0,
        tiled=True,
    )
    grad_share = jnp.sum(returned.reshape(groups, DEV_GROUP, row_count, pair_width), axis=1)
    grad_share = grad_share.transpose(1, 0, 2).reshape(row_count, groups * pair_width)
    empty_taps = jnp.zeros((conv_depth + 1, groups * pair_width), jnp.float32)
    grad_wx, grad_bias, grad_decay, grad_skip = lax.psum(
        (grad_wx, grad_bias, grad_decay, grad_skip), "exch"
    )
    placed = lax.dynamic_update_slice_in_dim(empty_taps, grad_wbc, my_group * pair_width, 1)
    grad_taps = lax.psum(placed, ("dp", "exch"))
    grad_x = grad_xr.reshape(tokens, channels).astype(jnp.bfloat16)
    grad_bc = grad_share.astype(jnp.bfloat16)
    grad_dt = grad_dtr.reshape(tokens, head_count).T.astype(jnp.bfloat16)
    grad_heads = jnp.stack([grad_bias, grad_decay, grad_skip])
    return (grad_x, grad_bc, grad_dt, grad_wx, grad_taps, grad_heads)


def solution(mesh):
    in_specs = (
        P("exch", "dp"),
        P(("exch", "dp"), None),
        P("dp", "exch"),
        P("exch", "dp"),
        P("exch", "dp", None, None),
        P("exch", None, "dp"),
        P("exch", None, None),
        P("exch"),
        P("exch"),
        P(None, "dp"),
        P(),
        P("dp"),
        P("dp"),
        P("dp"),
    )
    out_specs = (
        P("exch", "dp"),
        P(("exch", "dp"), None),
        P("dp", "exch"),
        P(None, "dp"),
        P(),
        P(None, "dp"),
    )
    return jax.shard_map(local, mesh=mesh, in_specs=in_specs, out_specs=out_specs, check_vma=False)
```

profile of v0, /device:TPU:0, one launch (start us, length us, event | category | flops | bytes accessed | tf_op | source)
XLA Modules:
  0.0 124.4 jit_solution(9123671219750444243)
XLA Ops:
  0.6 0.7 fusion.80
  1.4 0.6 copy-done.8
  2.3 0.7 copy.167
  3.0 6.3 %all-to-all-start = ((bf16[4,1,1]{2,1,0:T(2,128)(2,1)}), bf16[4,1,1]{2,1,0:T(2,128)(2,1)S(1)}, u32[]{:S(2)}, u32[]{:S(2)}) async-start(bf16[4,1,1]{2,1,0:T(2,128)(2,1)} %copy.167), calls=%async_computation | async-start | bytes 4096 | tf_op jit(solution)/shard_map/all_to_all | solution.py:127
  9.4 1.2 reshape.547
  12.8 0.7 copy-done.7
  14.2 0.7 reduce.16
  14.8 0.6 reshape.551
  15.7 0.7 reduce.17
  16.4 0.6 reshape.553
  17.4 0.6 copy-done.4
  18.1 9.3 %all_gather.3 = bf16[256,256]{1,0:T(8,128)(2,1)S(1)} all-gather(bf16[32,256]{1,0:T(8,128)(2,1)S(1)} %copy-done.4), channel_id=1, replica_groups=mesh['dp'=8,'exch'=4] {'dp'}, dimensions={0}, use_global_device_ids=true | all-gather | bytes 147456 | tf_op jit(solution)/shard_map/all_gather | solution.py:145
  27.8 1.0 reduce.18
  28.8 1.0 reshape.555
  29.8 0.9 copy-done.2
  31.1 5.1 %all-to-all-start.1 = ((bf16[4,2,384]{2,1,0:T(2,128)(2,1)}), bf16[4,2,384]{2,1,0:T(2,128)(2,1)S(1)}, u32[]{:S(2)}, u32[]{:S(2)}) async-start(bf16[4,2,384]{2,1,0:T(2,128)(2,1)} %reshape.553), calls=%async_computation.1 | async-start | bytes 12288 | tf_op jit(solution)/shard_map/all_to_all | solution.py:126
  36.6 5.2 %all-to-all-done.1 = bf16[4,2,384]{2,1,0:T(2,128)(2,1)S(1)} async-done(((bf16[4,2,384]{2,1,0:T(2,128)(2,1)}), bf16[4,2,384]{2,1,0:T(2,128)(2,1)S(1)}, u32[]{:S(2)}, u32[]{:S(2)}) %all-to-all-start.1) | async-done | bytes 6176 | tf_op jit(solution)/shard_map/all_to_all | solution.py:126
  41.8 3.2 %all-to-all-start.2 = ((bf16[4,2,384]{2,1,0:T(2,128)(2,1)}), bf16[4,2,384]{2,1,0:T(2,128)(2,1)S(1)}, u32[]{:S(2)}, u32[]{:S(2)}) async-start(bf16[4,2,384]{2,1,0:T(2,128)(2,1)} %reshape.551), calls=%async_computation.2 | async-start | bytes 12288 | tf_op jit(solution)/shard_map/all_to_all | solution.py:125
  45.3 5.4 %all-to-all-done.2 = bf16[4,2,384]{2,1,0:T(2,128)(2,1)S(1)} async-done(((bf16[4,2,384]{2,1,0:T(2,128)(2,1)}), bf16[4,2,384]{2,1,0:T(2,128)(2,1)S(1)}, u32[]{:S(2)}, u32[]{:S(2)}) %all-to-all-start.2) | async-done | bytes 6176 | tf_op jit(solution)/shard_map/all_to_all | solution.py:125
  50.6 3.4 %all-to-all-start.3 = ((bf16[4,2,16384]{2,1,0:T(2,128)(2,1)}), bf16[4,2,16384]{2,1,0:T(2,128)(2,1)S(1)}, u32[]{:S(2)}, u32[]{:S(2)}) async-start(bf16[4,2,16384]{2,1,0:T(2,128)(2,1)} %reshape.555), calls=%async_computation.3 | async-start | bytes 524288 | tf_op jit(solution)/shard_map/all_to_all | solution.py:124
  55.3 1.3 %fusion.10 = (f32[2,128,4]{1,2,0:T(4,128)S(1)}, f32[2,128,4]{1,2,0:T(4,128)S(1)}, f32[2,128,128]{2,1,0:T(8,128)S(1)}) fusion(f32[2,128,128]{2,1,0:T(8,128)S(1)} %fusion.46, f32[128,128]{1,0:T(8,128)S(1)} %fusion.52, f32[2,128,4]{1,2,0:T(4,128)S(1)} %copy.171, pred[128,128]{1,0:T(8,128)(4,1)S(1)} %broadcast_compare_fusion, ...), kind=kOutput, calls=%fused_computation.27 | convolution fusion | flops 102201344 | bytes 885760 | tf_op jit(solution)/shard_map/transpose(jvp(rntsh,rnshp->rnthp))/dot_general | solution.py:38
  56.6 0.7 copy-done.12
  57.3 0.8 multiply_reduce_fusion.10
  59.0 0.7 fusion.19
  62.1 0.6 convolution_bitcast_fusion.2
  63.4 39.4 %psum.36 = f32[4,256]{1,0:T(4,128)} all-reduce(f32[4,256]{1,0:T(4,128)S(1)} %pad_add_fusion.6), channel_id=1, replica_groups=mesh['dp'=8,'exch'=4] {'dp','exch'}, use_global_device_ids=true, to_apply=%region_21.22 | all-reduce | flops 1024 | bytes 8192 | tf_op jit(solution)/shard_map/psum | solution.py:197
  102.9 2.2 %reduce_window_sum.46 = f32[2,1,128,4]{3,2,1,0:T(8,128)S(1)} reduce-window(f32[2,1,128,4]{3,2,1,0:T(8,128)S(1)} %bitcast_add_fusion, f32[]{:T(128)} %constant.56.clone.1), window={size=1x1x128x1 pad=0_0x0_0x0_127x0_0}, to_apply=%region_11.12 | reduce-window | flops 130048 | bytes 8196 | tf_op jit(solution)/shard_map/transpose(jvp(jit(cumsum)))/reduce_window_sum | solution.py:31
  105.2 0.8 multiply_reduce_fusion.11
  106.1 0.8 pad_add_fusion
  106.9 4.8 %all-to-all-start.4 = ((f32[8,32,256]{2,1,0:T(8,128)}), f32[8,32,256]{2,1,0:T(8,128)S(1)}, u32[]{:S(2)}, u32[]{:S(2)}) async-start(f32[8,32,256]{2,1,0:T(8,128)} %bitcast.44), calls=%async_computation.4 | async-start | bytes 524288 | tf_op jit(solution)/shard_map/all_to_all | solution.py:183
  111.9 11.3 %all-reduce.18 = (f32[4,256]{1,0:T(4,128)}, f32[1,4]{1,0:T(1,128)S(1)}, f32[1,4]{1,0:T(1,128)S(1)}, f32[1,4]{1,0:T(1,128)S(1)}) all-reduce(f32[4,256]{1,0:T(4,128)S(1)} %pad_add_fusion.7, f32[1,4]{1,0:T(1,128)S(1)} %bitcast.233, f32[1,4]{1,0:T(1,128)S(1)} %multiply_bitcast_fusion, ...), channel_id=1, replica_groups=mesh['dp'=8,'exch'=4] {'exch'}, use_global_device_ids=true, to_apply=%region_16.17 | all-reduce | flops 1036 | bytes 8288 | tf_op jit(solution)/shard_map/psum | solution.py:193
  123.8 0.6 reduce_sum.196
  (93 shorter events, 11.4 us)
Async XLA Ops:
  0.6 12.8 %copy-start = (bf16[2,3,256]{2,0,1:T(2,128)(2,1)S(1)}, bf16[2,3,256]{2,0,1:T(2,128)(2,1)}, u32[]{:S(2)}) copy-start(bf16[2,3,256]{2,0,1:T(2,128)(2,1)} %param.19) | copy-start | bytes 9220
  1.4 0.7 copy-start.8
  3.0 28.1 %all-to-all-start = ((bf16[4,1,1]{2,1,0:T(2,128)(2,1)}), bf16[4,1,1]{2,1,0:T(2,128)(2,1)S(1)}, u32[]{:S(2)}, u32[]{:S(2)}) async-start(bf16[4,1,1]{2,1,0:T(2,128)(2,1)} %copy.167), calls=%async_computation | async-start | bytes 4096 | tf_op jit(solution)/shard_map/all_to_all | solution.py:127
  9.4 1.2 copy-start.1
  10.6 0.7 copy-start.13
  10.7 0.7 copy-start.11
  11.3 0.7 copy-start.3
  11.3 0.7 copy-start.5
  12.1 0.7 copy-start.6
  12.8 0.7 copy-start.7
  14.8 0.7 copy-start.10
  17.3 0.7 copy-start.4
  18.0 9.4 %copy-start.9 = (bf16[2,4,64,128]{3,2,1,0:T(8,128)(2,1)S(1)}, bf16[2,4,64,128]{3,2,1,0:T(8,128)(2,1)}, u32[]{:S(2)}) copy-start(bf16[2,4,64,128]{3,2,1,0:T(8,128)(2,1)} %param.18) | copy-start | bytes 393220
  29.8 0.9 copy-start.2
  31.1 10.7 %all-to-all-start.1 = ((bf16[4,2,384]{2,1,0:T(2,128)(2,1)}), bf16[4,2,384]{2,1,0:T(2,128)(2,1)S(1)}, u32[]{:S(2)}, u32[]{:S(2)}) async-start(bf16[4,2,384]{2,1,0:T(2,128)(2,1)} %reshape.553), calls=%async_computation.1 | async-start | bytes 12288 | tf_op jit(solution)/shard_map/all_to_all | solution.py:126
  41.8 8.8 %all-to-all-start.2 = ((bf16[4,2,384]{2,1,0:T(2,128)(2,1)}), bf16[4,2,384]{2,1,0:T(2,128)(2,1)S(1)}, u32[]{:S(2)}, u32[]{:S(2)}) async-start(bf16[4,2,384]{2,1,0:T(2,128)(2,1)} %reshape.551), calls=%async_computation.2 | async-start | bytes 12288 | tf_op jit(solution)/shard_map/all_to_all | solution.py:125
  50.6 10.2 %all-to-all-start.3 = ((bf16[4,2,16384]{2,1,0:T(2,128)(2,1)}), bf16[4,2,16384]{2,1,0:T(2,128)(2,1)S(1)}, u32[]{:S(2)}, u32[]{:S(2)}) async-start(bf16[4,2,16384]{2,1,0:T(2,128)(2,1)} %reshape.555), calls=%async_computation.3 | async-start | bytes 524288 | tf_op jit(solution)/shard_map/all_to_all | solution.py:124
  56.6 0.7 copy-start.12
  106.9 16.9 %all-to-all-start.4 = ((f32[8,32,256]{2,1,0:T(8,128)}), f32[8,32,256]{2,1,0:T(8,128)S(1)}, u32[]{:S(2)}, u32[]{:S(2)}) async-start(f32[8,32,256]{2,1,0:T(8,128)} %bitcast.44), calls=%async_computation.4 | async-start | bytes 524288 | tf_op jit(solution)/shard_map/all_to_all | solution.py:183
where the time goes:
time: 125 us; the launch traced here: 124 us
  blocking collectives  60.1 us (48%)
  starting transfers between devices  22.9 us (18%)
  local copies, waits for them, and re-layouts  12.2 us (10%)
  other arithmetic  11.7 us (9%)
  waiting for transfers between devices  11.2 us (9%)
  matrix products  5.42 us (4%)
    psum x1, blocking collectives, local(): grad_taps = lax.psum(placed, ('dp', 'exch'))  39.4 us
    psum x1, blocking collectives, local(): lax.psum((grad_wx, grad_bias, grad_decay, grad_skip), 'exch')  11.3 us
    all_gather x1, blocking collectives, local(): gathered = lax.all_gather(bc_raw, 'dp', axis=0, tiled=True)  9.34 us
    unnamed x37, local copies, waits for them, and re-layouts  7.99 us
    all_to_all x1, starting transfers between devices, local(): lax.all_to_all(filled, 'exch', split_axis=0, concat_axis=0, tiled=True)  6.35 us
    all_to_all x1, waiting for transfers between devices, local(): lax.all_to_all(pack_slots(conv_x_state), 'exch', split_axis=0, concat_axi...  5.35 us
    all_to_all x1, waiting for transfers between devices, local(): lax.all_to_all(pack_slots(bc_state), 'exch', split_axis=0, concat_axis=0,...  5.23 us
    all_to_all x1, starting transfers between devices, local(): lax.all_to_all(pack_slots(bc_state), 'exch', split_axis=0, concat_axis=0,...  5.11 us
  transfers between devices with their start and end apart: 5, of which 3 were waited for; matrix products, arithmetic and copies ran while one was open for 12% of the time, Pallas kernels for 0%

commit v1 on v0

v1 whole, which is shorter than its diff:
```python
import functools

import jax
import jax.numpy as jnp
from jax import lax
from jax.experimental import pallas as pl
from jax.experimental.pallas import tpu as pltpu
from jax.sharding import PartitionSpec as P

DEV_GROUP = 8
GROUP = 1
MESH = pl.DeviceIdType.MESH
F32 = jnp.float32
BF16 = jnp.bfloat16


def nn(a, b):
    return lax.dot_general(a, b, (((1,), (0,)), ((), ())), preferred_element_type=F32)


def nt(a, b):
    return lax.dot_general(a, b, (((1,), (1,)), ((), ())), preferred_element_type=F32)


def split(a):
    high = a.astype(BF16)
    return high, (a - high.astype(F32)).astype(BF16)


def three(dot, a, b):
    return dot(a[0], b[0]) + (dot(a[0], b[1]) + dot(a[1], b[0]))


def iota(shape, dim):
    return lax.broadcasted_iota(jnp.int32, shape, dim)


def kernel(
    peers, slices, groups, owner, lens, bias, a_log, skip, x_ref, bc_ref, dt_ref, cot_ref,
    ssm_ref, cx_ref, cbc_ref, wx_ref, wbc_ref,
    gx_ref, gbc_ref, gdt_ref, gwx_ref, gtaps_ref, gheads_ref,
    msg, state, gath, msg_out, state_out, pad_x, pad_bc, dpx, dpbc, dw_ref, taps, raw, back,
    fin, sem_msg, sem_state, sem_gath, sem_taps, sem_back, sem_fin,
):
    mine = lax.axis_index("exch")
    me = lax.axis_index("dp")
    prompts, depth, channels = cx_ref.shape
    taps_n = depth + 1
    responses = lens.shape[0]
    heads = bias.shape[0]
    width = channels // heads
    tokens = x_ref.shape[0]
    length = tokens // responses
    rows = bc_ref.shape[0]
    pair = cbc_ref.shape[2]
    half = pair // 2
    lanes = responses * heads
    base = 8 - depth

    def along(offset):
        return {"exch": lax.rem(mine + offset, peers)}

    def across(offset):
        return {"dp": lax.rem(me + offset, slices)}

    barrier = pltpu.get_barrier_semaphore()
    for offset in range(1, slices):
        pl.semaphore_signal(barrier, inc=1, device_id=across(offset), device_id_type=MESH)
    for offset in range(1, peers):
        pl.semaphore_signal(barrier, inc=1, device_id=along(offset), device_id_type=MESH)

    def fill(target, msg_dst, state_dst):
        small = jnp.zeros((depth, channels + pair), F32)
        flag = jnp.zeros((1, channels + pair), F32)
        big = jnp.zeros(ssm_ref.shape[1:], F32)
        for p in range(prompts):
            weight = (owner[p] == target).astype(F32)
            both = jnp.concatenate([cx_ref[p].astype(F32), cbc_ref[p].astype(F32)], axis=1)
            small = small + both * weight
            flag = flag + weight
            big = big + ssm_ref[p].astype(F32) * weight
        msg_dst[0:depth] = small
        msg_dst[depth : depth + 1] = flag
        state_dst[...] = big.astype(BF16)

    for offset in range(1, peers):
        fill(lax.rem(mine + offset, peers), msg_out.at[offset], state_out.at[offset])
    fill(mine, msg.at[mine], state.at[mine])

    pl.semaphore_wait(barrier, slices - 1 + peers - 1)

    def remote(src, dst, sem, offset, where):
        copy = pltpu.make_async_remote_copy(
            src_ref=src,
            dst_ref=dst,
            send_sem=sem.at[0, offset],
            recv_sem=sem.at[1, offset],
            device_id=where,
            device_id_type=MESH,
        )
        copy.start()
        return copy

    def group_columns(ref, who):
        if groups == 1:
            return ref
        start = pl.multiple_of((who // DEV_GROUP) * pair, pair)
        return ref.at[:, pl.ds(start, pair)]

    msg_copies = [
        remote(msg_out.at[o], msg.at[mine], sem_msg, o, along(o)) for o in range(1, peers)
    ]
    gath_copies = [
        remote(
            group_columns(bc_ref, lax.rem(me + o, slices)),
            gath.at[me],
            sem_gath,
            o,
            across(o),
        )
        for o in range(1, slices)
    ]
    state_copies = [
        remote(state_out.at[o], state.at[mine], sem_state, o, along(o))
        for o in range(peers - 1, 0, -1)
    ]
    gath[me] = group_columns(bc_ref, me)[...]

    row_head = lax.rem(iota((lanes, 1), 0), heads)

    def per_row(ref):
        out = jnp.zeros((lanes, 1), F32)
        for h in range(heads):
            out = jnp.where(row_head == h, ref[h], out)
        return out

    lane_head = iota((1, channels), 1) // width
    skip_row = jnp.zeros((1, channels), F32)
    for h in range(heads):
        skip_row = jnp.where(lane_head == h, skip[h], skip_row)
    dt_in = jnp.concatenate(
        [dt_ref[:, r * length : (r + 1) * length].astype(F32) for r in range(responses)], axis=0
    )
    dt_pre = dt_in + per_row(bias)
    small = jnp.exp(-jnp.abs(dt_pre))
    above = 1.0 + small
    log1p = jnp.where(above == 1.0, small, jnp.log(above) * (small / (above - 1.0)))
    dt = jnp.maximum(dt_pre, 0.0) + log1p
    rate = jnp.exp(per_row(a_log))
    first = iota((length, length), 0)
    second = iota((length, length), 1)
    upto = (first <= second).astype(F32)
    onward = (first >= second).astype(F32)
    causal = first <= second
    logs = lax.dot_general(
        -rate * dt,
        upto,
        (((1,), (0,)), ((), ())),
        preferred_element_type=F32,
        precision=lax.Precision.HIGHEST,
    )
    entry = jnp.exp(logs)
    logs_col = logs.T
    dt_col = dt.T
    entry_col = entry.T

    def spread_heads(cols, r):
        parts = [
            jnp.broadcast_to(cols[:, r * heads + h : r * heads + h + 1], (length, width))
            for h in range(heads)
        ]
        return jnp.concatenate(parts, axis=1)

    def indicator(r):
        row = iota((lanes, channels), 0)
        head = iota((lanes, channels), 1) // width
        return (row == r * heads + head).astype(BF16)

    for r in range(responses):
        block = slice(r * length, (r + 1) * length)
        pad_x[r, 8 : 8 + length] = x_ref[block].astype(F32)
    cots = []
    for r in range(responses):
        block = slice(r * length, (r + 1) * length)
        live = iota((length, 1), 0) < lens[r]
        cots.append(jnp.where(live, cot_ref[block].astype(F32), 0.0))

    for copy in msg_copies:
        copy.wait_recv()
    weights = [[None] * peers for _ in range(prompts)]
    seen = jnp.zeros((1, channels + pair), F32)
    for z in range(peers):
        present = msg[z, depth : depth + 1]
        for j in range(prompts):
            weights[j][z] = jnp.where(seen == float(j), present, 0.0)
        seen = seen + present
    for r in range(responses):
        prev = jnp.zeros((depth, channels + pair), F32)
        for z in range(peers):
            prev = prev + msg[z, 0:depth] * weights[r // GROUP][z]
        pad_x[r, base:8] = prev[:, :channels]
        pad_bc[r, base:8] = prev[:, channels:]

    def convolve(pad, weight, r):
        pre = pad[r, base : base + length] * weight[0:1]
        for k in range(1, taps_n):
            pre = pre + pad[r, base + k : base + k + length] * weight[k : k + 1]
        gate = 1.0 / (1.0 + jnp.exp(-pre))
        return pre * gate, gate * (1.0 + pre * (1.0 - gate))

    wx = wx_ref[...]
    wbc = wbc_ref[...]
    x_acts = [convolve(pad_x, wx, r) for r in range(responses)]

    for copy in gath_copies:
        copy.wait_recv()
    slots = length // rows
    for d in range(slices):
        r, place = d // slots, d % slots
        pad_bc[r, 8 + place * rows : 8 + (place + 1) * rows] = gath[d].astype(F32)
    bc_acts = [convolve(pad_bc, wbc, r) for r in range(responses)]

    across_rows = jnp.zeros((lanes, length), F32)
    dt_first = jnp.zeros((lanes, length), F32)
    row_index = iota((lanes, 1), 0)
    skip_sum = jnp.zeros((1, channels), F32)
    grad_wx = jnp.zeros((taps_n, channels), F32)
    b_grads, c_grads = [], []

    def weight_grad(grad, pad, r):
        parts = [
            jnp.sum(grad * pad[r, base + k : base + k + length], axis=0, keepdims=True)
            for k in range(taps_n)
        ]
        return jnp.concatenate(parts, axis=0)

    def input_grad(ref, weight, r):
        total = ref[r, depth : depth + length] * weight[0:1]
        for k in range(1, taps_n):
            total = total + ref[r, depth - k : depth - k + length] * weight[k : k + 1]
        return total

    for r in range(responses):
        act, slope = x_acts[r]
        cot = cots[r]
        cot_b = cot.astype(BF16)
        dt_full = spread_heads(dt_col, r)
        weighted = split(act * dt_full)
        proj_b = split(bc_acts[r][0][:, :half])
        proj_c = split(bc_acts[r][0][:, half:])
        scores = three(nt, proj_b, proj_c)
        score_grad = jnp.zeros((length, length), F32)
        for h in range(heads):
            i = r * heads + h
            cols = slice(h * width, (h + 1) * width)
            cot_h = cot_b[:, cols]
            gap = logs[i : i + 1] - logs_col[:, i : i + 1]
            decay = jnp.where(causal, jnp.exp(jnp.where(causal, gap, 0.0)), 0.0)
            mix = scores * decay
            mix_grad = nt(weighted[0][:, cols], cot_h) + nt(weighted[1][:, cols], cot_h)
            high, low = split(mix)
            dw_ref[r, :, cols] = nn(high, cot_h) + nn(low, cot_h)
            score_grad = score_grad + mix_grad * decay
            found = jnp.sum(mix_grad * mix, axis=0, keepdims=True)
            across_rows = jnp.where(row_index == i, found, across_rows)
        dw = dw_ref[r]
        prod = split(dw * act)
        mark = indicator(r)
        dt_first = dt_first + (nt(mark, prod[0]) + nt(mark, prod[1]))
        skip_sum = skip_sum + jnp.sum(cot * act, axis=0, keepdims=True)
        pre_grad = (dw * dt_full + skip_row * cot) * slope
        dpx[r, 0:length] = pre_grad
        dpx[r, length : length + 8] = jnp.zeros((8, channels), F32)
        grad_wx = grad_wx + weight_grad(pre_grad, pad_x, r)
        gx_ref[r * length : (r + 1) * length] = input_grad(dpx, wx, r).astype(BF16)
        b_grads.append(three(nn, split(score_grad), proj_c))
        c_grads.append(three(nn, split(score_grad.T), proj_b))

    for copy in state_copies:
        copy.wait_recv()
    starts = []
    grad_taps = jnp.zeros((taps_n, pair), F32)
    for r in range(responses):
        start = jnp.zeros(state.shape[1:], F32)
        for z in range(peers):
            pick = weights[r // GROUP][z][:, : state.shape[2]]
            start = start + state[z].astype(F32) * pick
        start = start.astype(BF16)
        starts.append(start)
        fed = split(cots[r] * spread_heads(entry_col, r))
        c_grad = c_grads[r] + (nn(fed[0], start) + nn(fed[1], start))
        slope = bc_acts[r][1]
        pre_grad = jnp.concatenate([b_grads[r], c_grad], axis=1) * slope
        dpbc[r, 0:length] = pre_grad
        dpbc[r, length : length + 8] = jnp.zeros((8, pair), F32)
        grad_taps = grad_taps + weight_grad(pre_grad, pad_bc, r)

    taps[me, 0:taps_n] = grad_taps
    taps_copies = [
        remote(taps.at[me], taps.at[me], sem_taps, o, across(o)) for o in range(1, slices)
    ]
    for r in range(responses):
        block = input_grad(dpbc, wbc, r)
        for place in range(slots):
            raw[r * slots + place] = block[place * rows : (place + 1) * rows]
    back_copies = [
        remote(raw.at[lax.rem(me + o, slices)], back.at[me], sem_back, o, across(o))
        for o in range(1, slices)
    ]
    back[me] = raw[me]

    entry_grad = jnp.zeros((lanes, length), F32)
    for r in range(responses):
        proj_c = split(bc_acts[r][0][:, half:])
        carried = nt(proj_c[0], starts[r]) + nt(proj_c[1], starts[r])
        prod = split(carried * cots[r])
        mark = indicator(r)
        entry_grad = entry_grad + (nt(mark, prod[0]) + nt(mark, prod[1]))
    log_grad = across_rows + entry * entry_grad - dt * dt_first
    step_grad = lax.dot_general(
        log_grad,
        onward,
        (((1,), (0,)), ((), ())),
        preferred_element_type=F32,
        precision=lax.Precision.HIGHEST,
    )
    dt_grad = dt_first - rate * step_grad
    raw_grad = dt_grad * (1.0 / (1.0 + jnp.exp(-dt_pre)))
    for r in range(responses):
        gdt_ref[:, r * length : (r + 1) * length] = raw_grad[
            r * heads : (r + 1) * heads
        ].astype(BF16)
    bias_rows = jnp.sum(raw_grad, axis=1, keepdims=True)
    decay_rows = -rate * jnp.sum(dt * step_grad, axis=1, keepdims=True)
    bias_grad = jnp.zeros((heads, 1), F32)
    decay_grad = jnp.zeros((heads, 1), F32)
    for r in range(responses):
        bias_grad = bias_grad + bias_rows[r * heads : (r + 1) * heads]
        decay_grad = decay_grad + decay_rows[r * heads : (r + 1) * heads]
    own = iota((heads, channels), 0) == iota((heads, channels), 1) // width
    skip_grad = jnp.sum(jnp.where(own, skip_sum, 0.0), axis=1, keepdims=True)
    column = iota((heads, half), 1)
    head_block = jnp.where(
        column == 0,
        bias_grad,
        jnp.where(column == 1, decay_grad, jnp.where(column == 2, skip_grad, 0.0)),
    )
    fin[mine, 0:taps_n, 0:channels] = grad_wx
    fin[mine, 8 : 8 + heads, 0:half] = head_block

    for copy in taps_copies:
        copy.wait_recv()
    for q in range(groups):
        total = taps[q * DEV_GROUP, 0:taps_n]
        for d in range(1, DEV_GROUP):
            total = total + taps[q * DEV_GROUP + d, 0:taps_n]
        fin[mine, 16 : 16 + taps_n, q * pair : (q + 1) * pair] = total
    fin_copies = [
        remote(fin.at[mine], fin.at[mine], sem_fin, o, along(o)) for o in range(1, peers)
    ]

    for copy in back_copies:
        copy.wait_recv()
    for q in range(groups):
        total = back[q * DEV_GROUP]
        for d in range(1, DEV_GROUP):
            total = total + back[q * DEV_GROUP + d]
        gbc_ref[:, q * pair : (q + 1) * pair] = total.astype(BF16)

    for copy in fin_copies:
        copy.wait_recv()
    wx_total = fin[0, 0:taps_n, 0:channels]
    head_total = fin[0, 8:16, 0:half]
    taps_total = fin[0, 16 : 16 + taps_n, 0 : groups * pair]
    for z in range(1, peers):
        wx_total = wx_total + fin[z, 0:taps_n, 0:channels]
        head_total = head_total + fin[z, 8:16, 0:half]
        taps_total = taps_total + fin[z, 16 : 16 + taps_n, 0 : groups * pair]
    gwx_ref[...] = wx_total
    gtaps_ref[...] = taps_total
    gheads_ref[...] = head_total.T[0:3, 0:heads]
    for copy in msg_copies + gath_copies + state_copies + taps_copies + back_copies + fin_copies:
        copy.wait_send()


def local(
    x_raw, bc_raw, dt_raw, cotangent, ssm_state, conv_x_state, conv_bc_state, owner, resp_len,
    conv_x_weight, conv_bc_weight, dt_bias, a_log, skip_d,
):
    peers = lax.axis_size("exch")
    slices = lax.axis_size("dp")
    prompts, heads, width, nstate = ssm_state.shape
    channels = x_raw.shape[1]
    pair = 2 * nstate
    depth = conv_x_state.shape[1]
    responses = resp_len.shape[0]
    tokens = x_raw.shape[0]
    length = tokens // responses
    rows, all_pairs = bc_raw.shape
    groups = all_pairs // pair
    bc_state, bc_weight = conv_bc_state, conv_bc_weight
    if groups > 1:
        first = (lax.axis_index("dp") // DEV_GROUP) * pair
        bc_state = lax.dynamic_slice_in_dim(conv_bc_state, first, pair, 2)
        bc_weight = lax.dynamic_slice_in_dim(conv_bc_weight, first, pair, 1)
    ssm = ssm_state.reshape(prompts, heads * width, nstate)
    wide = max(all_pairs, channels)
    vmem = pl.BlockSpec(memory_space=pltpu.VMEM)
    smem = pl.BlockSpec(memory_space=pltpu.SMEM)
    dma = pltpu.SemaphoreType.DMA
    outs = (
        jax.ShapeDtypeStruct((tokens, channels), BF16),
        jax.ShapeDtypeStruct((rows, all_pairs), BF16),
        jax.ShapeDtypeStruct((heads, tokens), BF16),
        jax.ShapeDtypeStruct((depth + 1, channels), F32),
        jax.ShapeDtypeStruct((depth + 1, all_pairs), F32),
        jax.ShapeDtypeStruct((3, heads), F32),
    )
    return pl.pallas_call(
        functools.partial(kernel, peers, slices, groups),
        out_shape=outs,
        in_specs=[smem] * 5 + [vmem] * 9,
        out_specs=[vmem] * 6,
        scratch_shapes=[
            pltpu.VMEM((peers, 8, channels + pair), F32),
            pltpu.VMEM((peers, heads * width, nstate), BF16),
            pltpu.VMEM((slices, rows, pair), BF16),
            pltpu.VMEM((peers, 8, channels + pair), F32),
            pltpu.VMEM((peers, heads * width, nstate), BF16),
            pltpu.VMEM((responses, length + 8, channels), F32),
            pltpu.VMEM((responses, length + 8, pair), F32),
            pltpu.VMEM((responses, length + 8, channels), F32),
            pltpu.VMEM((responses, length + 8, pair), F32),
            pltpu.VMEM((responses, length, channels), F32),
            pltpu.VMEM((slices, 8, pair), F32),
            pltpu.VMEM((slices, rows, pair), F32),
            pltpu.VMEM((slices, rows, pair), F32),
            pltpu.VMEM((peers, 24, wide), F32),
            dma((2, peers)),
            dma((2, peers)),
            dma((2, slices)),
            dma((2, slices)),
            dma((2, slices)),
            dma((2, peers)),
        ],
        compiler_params=pltpu.CompilerParams(collective_id=0, has_side_effects=True),
    )(
        owner, resp_len, dt_bias, a_log, skip_d, x_raw, bc_raw, dt_raw, cotangent, ssm,
        conv_x_state, bc_state, conv_x_weight, bc_weight,
    )


def solution(mesh):
    in_specs = (
        P("exch", "dp"),
        P(("exch", "dp"), None),
        P("dp", "exch"),
        P("exch", "dp"),
        P("exch", "dp", None, None),
        P("exch", None, "dp"),
        P("exch", None, None),
        P("exch"),
        P("exch"),
        P(None, "dp"),
        P(),
        P("dp"),
        P("dp"),
        P("dp"),
    )
    out_specs = (
        P("exch", "dp"),
        P(("exch", "dp"), None),
        P("dp", "exch"),
        P(None, "dp"),
        P(),
        P(None, "dp"),
    )
    return jax.shard_map(local, mesh=mesh, in_specs=in_specs, out_specs=out_specs, check_vma=False)
```

time: 125 us -> 32.5 us (0.26)
  blocking collectives: 60.1 us -> 0 us
  Pallas kernels: 0 us -> 24.8 us
  starting transfers between devices: 22.9 us -> 0 us
  other arithmetic: 11.7 us -> 0 us
  waiting for transfers between devices: 11.2 us -> 0 us
  local copies, waits for them, and re-layouts: 12.2 us -> 6.76 us
  matrix products: 5.42 us -> 0 us
    psum x2 -> x0, blocking collectives: 50.7 us -> none  [the longest x1 39.4 us: local(): grad_taps = lax.psum(placed, ('dp', 'exch'))]
    pallas_call x0 -> x1, Pallas kernels: none -> 24.8 us  [local(): pl.pallas_call(functools.partial(kernel, peers, slices, groups), out_shap...]
    all_to_all x5 -> x0, starting transfers between devices: 22.9 us -> none  [the longest x1 6.35 us: local(): lax.all_to_all(filled, 'exch', split_axis=0, concat_axis=0, tiled=True)]
    all_to_all x5 -> x0, waiting for transfers between devices: 11.2 us -> none  [the longest x1 5.35 us: local(): lax.all_to_all(pack_slots(conv_x_state), 'exch', split_axis=0, concat_axi...]
    all_gather x1 -> x0, blocking collectives: 9.34 us -> none  [local(): gathered = lax.all_gather(bc_raw, 'dp', axis=0, tiled=True)]
    dot_general x13 -> x0, matrix products: 5.42 us -> none  [the longest x2 2.06 us: ssd_output(): jnp.einsum('rntsh,rnshp->rnthp', mixing, weighted, precision=PRECISE)]
    another operation x7 -> x0, other arithmetic: 3.97 us -> none  [the longest x2 2.41 us: ssd_output(): logs = jnp.cumsum(-rate * step_blocks, axis=2)]
    reduce_sum x9 -> x0, other arithmetic: 2.74 us -> none  [the longest x1 0.8 us: ssd_output(): logs = jnp.cumsum(-rate * step_blocks, axis=2)]
  transfers between devices with their start and end apart: 5 -> 0, of which waited for: 3 -> 0; matrix products, arithmetic and copies ran while one was open for 12% -> 0% of each run, Pallas kernels for 0% -> 0%
where the time goes in v1:
time: 32.5 us; the launch traced here: 32.2 us
  Pallas kernels  24.8 us (76%)
  local copies, waits for them, and re-layouts  6.76 us (21%)
  between operations  0.66 us (2%)
    pallas_call x1, Pallas kernels, local(): pl.pallas_call(functools.partial(kernel, peers, slices, groups), out_shap...  24.8 us
    unnamed x20, local copies, waits for them, and re-layouts  6.76 us

profile of v1, /device:TPU:0, one launch (start us, length us, event | category | flops | bytes accessed | tf_op | source)
XLA Modules:
  0.0 32.2 jit_solution(16319443094409956153)
XLA Ops:
  0.6 0.0 copy-start.3
  0.6 1.3 %copy.20.cx_ref = bf16[2,3,256]{2,1,0:T(4,128)(2,1)} copy(bf16[2,3,256]{2,0,1:T(2,128)(2,1)} %param.19) | data formatting | bytes 6144 | tf_op args[5]
  1.9 0.0 copy-done.3
  1.9 0.6 %copy.21.cbc_ref = bf16[2,3,256]{2,1,0:T(4,128)(2,1)} copy(bf16[2,3,256]{2,0,1:T(2,128)(2,1)S(1)} %copy-done.3) | data formatting | bytes 6144 | tf_op args[6]
  2.5 24.8 %shard_map.181 = (bf16[256,256]{1,0:T(8,128)(2,1)}, bf16[32,256]{1,0:T(8,128)(2,1)}, bf16[4,256]{1,0:T(4,128)(2,1)}, f32[4,256]{1,0:T(4,128)}, f32[4,256]{1,0:T(4,128)}, /*index=5*/f32[3,4]{1,0:T(4,128)}) custom-call(s32[2]{0:T(128)} %owner.1, s32[2]{0:T(128)} %lens.1, f32[4]{0:T(128)} %bias.1, f32[4]{0:T(128)} %a_log.1, f32[4]{0:T(128)} %skip.1, ...), custom_call_target="tpu_custom_call" | custom-call | tf_op jit(solution)/shard_map/pallas_call | solution.py:419
  27.3 0.0 copy-start
  27.3 1.6 %copy.28 = bf16[256,256]{1,0:T(8,128)(2,1)} copy(bf16[256,256]{1,0:T(8,128)(2,1)} %get-tuple-element.12) | data formatting | bytes 262144
  28.9 0.0 copy-done
  28.9 0.0 copy-start.5
  28.9 0.6 %copy.29 = bf16[32,256]{1,0:T(8,128)(2,1)} copy(bf16[32,256]{1,0:T(8,128)(2,1)S(1)} %copy-done) | data formatting | bytes 32768
  29.5 0.1 copy-done.5
  29.6 0.0 copy-start.2
  29.6 0.6 %copy.30 = bf16[4,256]{1,0:T(4,128)(2,1)} copy(bf16[4,256]{1,0:T(4,128)(2,1)S(1)} %copy-done.5) | data formatting | bytes 4096
  30.2 0.1 copy-done.2
  30.2 0.0 copy-start.1
  30.2 0.6 %copy.31 = f32[4,256]{1,0:T(4,128)} copy(f32[4,256]{1,0:T(4,128)S(1)} %copy-done.2) | data formatting | bytes 8192
  30.8 0.1 copy-done.1
  30.9 0.0 copy-start.4
  30.9 0.6 %copy.32 = f32[4,256]{1,0:T(4,128)} copy(f32[4,256]{1,0:T(4,128)S(1)} %copy-done.1) | data formatting | bytes 8192
  31.5 0.1 copy-done.4
  31.6 0.6 %copy.33 = f32[3,4]{1,0:T(4,128)} copy(f32[3,4]{1,0:T(4,128)S(1)} %copy-done.4) | data formatting | bytes 96
Async XLA Ops:
  0.6 1.3 %copy-start.3 = (bf16[2,3,256]{2,0,1:T(2,128)(2,1)S(1)}, bf16[2,3,256]{2,0,1:T(2,128)(2,1)}, u32[]{:S(2)}) copy-start(bf16[2,3,256]{2,0,1:T(2,128)(2,1)} %param.20) | copy-start | bytes 9220
  27.3 1.6 %copy-start = (bf16[32,256]{1,0:T(8,128)(2,1)S(1)}, bf16[32,256]{1,0:T(8,128)(2,1)}, u32[]{:S(2)}) copy-start(bf16[32,256]{1,0:T(8,128)(2,1)} %get-tuple-element.13) | copy-start | bytes 49156
  28.9 0.7 %copy-start.5 = (bf16[4,256]{1,0:T(4,128)(2,1)S(1)}, bf16[4,256]{1,0:T(4,128)(2,1)}, u32[]{:S(2)}) copy-start(bf16[4,256]{1,0:T(4,128)(2,1)} %get-tuple-element.14) | copy-start | bytes 6148
  29.6 0.7 %copy-start.2 = (f32[4,256]{1,0:T(4,128)S(1)}, f32[4,256]{1,0:T(4,128)}, u32[]{:S(2)}) copy-start(f32[4,256]{1,0:T(4,128)} %get-tuple-element.15) | copy-start | bytes 12292
  30.2 0.7 %copy-start.1 = (f32[4,256]{1,0:T(4,128)S(1)}, f32[4,256]{1,0:T(4,128)}, u32[]{:S(2)}) copy-start(f32[4,256]{1,0:T(4,128)} %get-tuple-element.16) | copy-start | bytes 12292
  30.9 0.7 %copy-start.4 = (f32[3,4]{1,0:T(4,128)S(1)}, f32[3,4]{1,0:T(4,128)}, u32[]{:S(2)}) copy-start(f32[3,4]{1,0:T(4,128)} %get-tuple-element.17) | copy-start | bytes 148

commit v2 on v1

--- a/solution.py
+++ b/solution.py
@@ -36,15 +36,20 @@
 
 
 def kernel(
-    peers, slices, groups, owner, lens, bias, a_log, skip, x_ref, bc_ref, dt_ref, cot_ref,
-    ssm_ref, cx_ref, cbc_ref, wx_ref, wbc_ref,
-    gx_ref, gbc_ref, gdt_ref, gwx_ref, gtaps_ref, gheads_ref,
+    peers, slices, groups, *refs
+):
+    sources, refs = refs[:14], refs[14:]
+    gx_ref, gbc_ref, gdt_ref, fin = refs[:4]
+    inputs, refs = refs[4:18], refs[18:]
+    owner, lens, bias, a_log, skip, x_ref, bc_ref, dt_ref, cot_ref = inputs[:9]
+    ssm_ref, cx_ref, cbc_ref, wx_ref, wbc_ref = inputs[9:]
+    (
     msg, state, gath, msg_out, state_out, pad_x, pad_bc, dpx, dpbc, dw_ref, taps, raw, back,
-    fin, sem_msg, sem_state, sem_gath, sem_taps, sem_back, sem_fin,
-):
+    sem_in, sem_msg, sem_state, sem_gath, sem_taps, sem_back, sem_fin,
+    ) = refs
     mine = lax.axis_index("exch")
     me = lax.axis_index("dp")
-    prompts, depth, channels = cx_ref.shape
+    depth, prompts, channels = cx_ref.shape
     taps_n = depth + 1
     responses = lens.shape[0]
     heads = bias.shape[0]
@@ -69,17 +74,36 @@
     for offset in range(1, peers):
         pl.semaphore_signal(barrier, inc=1, device_id=along(offset), device_id_type=MESH)
 
+    loads = [
+        pltpu.make_async_copy(src, dst, sem_in.at[i])
+        for i, (src, dst) in enumerate(zip(sources, inputs))
+    ]
+    sooner = (0, 10, 11, 9, 6)
+    later = [i for i in range(len(loads)) if i not in sooner]
+    for i in sooner:
+        loads[i].start()
+    for i in later:
+        loads[i].start()
+    for i in sooner:
+        loads[i].wait()
+
+    tails = [
+        jnp.concatenate([cx_ref[k].astype(F32), cbc_ref[k].astype(F32)], axis=1)
+        for k in range(depth)
+    ]
+
     def fill(target, msg_dst, state_dst):
-        small = jnp.zeros((depth, channels + pair), F32)
+        small = [jnp.zeros((1, channels + pair), F32)] * depth
         flag = jnp.zeros((1, channels + pair), F32)
         big = jnp.zeros(ssm_ref.shape[1:], F32)
         for p in range(prompts):
             weight = (owner[p] == target).astype(F32)
-            both = jnp.concatenate([cx_ref[p].astype(F32), cbc_ref[p].astype(F32)], axis=1)
-            small = small + both * weight
+            for k in range(depth):
+                small[k] = small[k] + tails[k][p : p + 1] * weight
             flag = flag + weight
             big = big + ssm_ref[p].astype(F32) * weight
-        msg_dst[0:depth] = small
+        for k in range(depth):
+            msg_dst[k : k + 1] = small[k]
         msg_dst[depth : depth + 1] = flag
         state_dst[...] = big.astype(BF16)
 
@@ -125,6 +149,9 @@
         for o in range(peers - 1, 0, -1)
     ]
     gath[me] = group_columns(bc_ref, me)[...]
+
+    for i in later:
+        loads[i].wait()
 
     row_head = lax.rem(iota((lanes, 1), 0), heads)
 
@@ -345,6 +372,7 @@
         bias_grad,
         jnp.where(column == 1, decay_grad, jnp.where(column == 2, skip_grad, 0.0)),
     )
+    fin[mine] = jnp.zeros(fin.shape[1:], F32)
     fin[mine, 0:taps_n, 0:channels] = grad_wx
     fin[mine, 8 : 8 + heads, 0:half] = head_block
 
@@ -369,18 +397,32 @@
 
     for copy in fin_copies:
         copy.wait_recv()
-    wx_total = fin[0, 0:taps_n, 0:channels]
-    head_total = fin[0, 8:16, 0:half]
-    taps_total = fin[0, 16 : 16 + taps_n, 0 : groups * pair]
-    for z in range(1, peers):
-        wx_total = wx_total + fin[z, 0:taps_n, 0:channels]
-        head_total = head_total + fin[z, 8:16, 0:half]
-        taps_total = taps_total + fin[z, 16 : 16 + taps_n, 0 : groups * pair]
-    gwx_ref[...] = wx_total
-    gtaps_ref[...] = taps_total
-    gheads_ref[...] = head_total.T[0:3, 0:heads]
     for copy in msg_copies + gath_copies + state_copies + taps_copies + back_copies + fin_copies:
         copy.wait_send()
+
+
+def finish(
+    gx_in, gbc_in, gdt_in, fin, gx_ref, gbc_ref, gdt_ref, gwx_ref, gtaps_ref, gheads_ref, sems
+):
+    copies = [
+        pltpu.make_async_copy(src, dst, sems.at[i])
+        for i, (src, dst) in enumerate(
+            ((gx_in, gx_ref), (gbc_in, gbc_ref), (gdt_in, gdt_ref))
+        )
+    ]
+    for copy in copies:
+        copy.start()
+    taps_n, channels = gwx_ref.shape
+    heads = gheads_ref.shape[1]
+    pairs = gtaps_ref.shape[1]
+    total = fin[0]
+    for z in range(1, fin.shape[0]):
+        total = total + fin[z]
+    gwx_ref[...] = total[0:taps_n, 0:channels]
+    gtaps_ref[...] = total[16 : 16 + taps_n, 0:pairs]
+    gheads_ref[...] = total[8:16, 0:128].T[0:3, 0:heads]
+    for copy in copies:
+        copy.wait()
 
 
 def local(
@@ -406,7 +448,6 @@
     ssm = ssm_state.reshape(prompts, heads * width, nstate)
     wide = max(all_pairs, channels)
     vmem = pl.BlockSpec(memory_space=pltpu.VMEM)
-    smem = pl.BlockSpec(memory_space=pltpu.SMEM)
     dma = pltpu.SemaphoreType.DMA
     outs = (
         jax.ShapeDtypeStruct((tokens, channels), BF16),
@@ -416,12 +457,20 @@
         jax.ShapeDtypeStruct((depth + 1, all_pairs), F32),
         jax.ShapeDtypeStruct((3, heads), F32),
     )
-    return pl.pallas_call(
+    staged = tuple(pltpu.VMEM(out.shape, out.dtype) for out in outs[:3])
+    staged = staged + (pltpu.VMEM((peers, 24, wide), F32),)
+    args = (
+        owner, resp_len, dt_bias, a_log, skip_d, x_raw, bc_raw, dt_raw, cotangent, ssm,
+        conv_x_state.transpose(1, 0, 2), bc_state.transpose(1, 0, 2), conv_x_weight, bc_weight,
+    )
+    held = pl.pallas_call(
         functools.partial(kernel, peers, slices, groups),
-        out_shape=outs,
-        in_specs=[smem] * 5 + [vmem] * 9,
-        out_specs=[vmem] * 6,
-        scratch_shapes=[
+        out_shape=staged,
+        in_specs=[pl.BlockSpec(memory_space=pltpu.HBM)] * 14,
+        out_specs=[vmem] * 4,
+        scratch_shapes=[pltpu.SMEM(a.shape, a.dtype) for a in args[:5]]
+        + [pltpu.VMEM(a.shape, a.dtype) for a in args[5:]]
+        + [
             pltpu.VMEM((peers, 8, channels + pair), F32),
             pltpu.VMEM((peers, heads * width, nstate), BF16),
             pltpu.VMEM((slices, rows, pair), BF16),
@@ -435,7 +484,7 @@
             pltpu.VMEM((slices, 8, pair), F32),
             pltpu.VMEM((slices, rows, pair), F32),
             pltpu.VMEM((slices, rows, pair), F32),
-            pltpu.VMEM((peers, 24, wide), F32),
+            dma((14,)),
             dma((2, peers)),
             dma((2, peers)),
             dma((2, slices)),
@@ -443,11 +492,19 @@
             dma((2, slices)),
             dma((2, peers)),
         ],
-        compiler_params=pltpu.CompilerParams(collective_id=0, has_side_effects=True),
-    )(
-        owner, resp_len, dt_bias, a_log, skip_d, x_raw, bc_raw, dt_raw, cotangent, ssm,
-        conv_x_state, bc_state, conv_x_weight, bc_weight,
-    )
+        compiler_params=pltpu.CompilerParams(
+            collective_id=0, has_side_effects=True
+        ),
+    )(*args)
+    anywhere = pl.BlockSpec(memory_space=pl.ANY)
+    return pl.pallas_call(
+        finish,
+        out_shape=outs,
+        in_specs=[vmem] * 4,
+        out_specs=[anywhere] * 3 + [vmem] * 3,
+        scratch_shapes=[dma((3,))],
+        compiler_params=pltpu.CompilerParams(vmem_limit_bytes=16 * 1024 * 1024),
+    )(*held)
 
 
 def solution(mesh):

time: 32.5 us -> 25.1 us (0.77)
  local copies, waits for them, and re-layouts: 6.76 us -> 0 us
  Pallas kernels: 24.8 us -> 24.3 us
    unnamed x20 -> x0, local copies, waits for them, and re-layouts: 6.76 us -> none
    pallas_call x1, Pallas kernels: 24.8 us -> 23.1 us  [local(): pl.pallas_call(functools.partial(kernel, peers, slices, groups), out_shap...]
    pallas_call x0 -> x1, Pallas kernels: none -> 1.29 us  [local(): pl.pallas_call(finish, out_shape=outs, in_specs=[vmem] * 4, out_specs=[an...]
where the time goes in v2:
time: 25.1 us; the launch traced here: 25 us
  Pallas kernels  24.3 us (97%)
  between operations  0.65 us (3%)
    pallas_call x1, Pallas kernels, local(): pl.pallas_call(functools.partial(kernel, peers, slices, groups), out_shap...  23.1 us
    pallas_call x1, Pallas kernels, local(): pl.pallas_call(finish, out_shape=outs, in_specs=[vmem] * 4, out_specs=[an...  1.29 us

profile of v2, /device:TPU:0, one launch (start us, length us, event | category | flops | bytes accessed | tf_op | source)
XLA Modules:
  0.0 25.0 jit_solution(17985537858909622270)
XLA Ops:
  0.6 23.1 %shard_map.181 = (bf16[256,256]{1,0:T(8,128)(2,1)S(1)}, bf16[32,256]{1,0:T(8,128)(2,1)S(1)}, bf16[4,256]{1,0:T(4,128)(2,1)S(1)}, f32[4,24,256]{2,1,0:T(8,128)S(1)}) custom-call(s32[2]{0:T(128)} %refs_0_.1, s32[2]{0:T(128)} %refs_1_.1, f32[4]{0:T(128)} %refs_2_.1, f32[4]{0:T(128)} %refs_3_.1, f32[4]{0:T(128)} %refs_4_.1, bf16[256,256]{1,0:T(8,128)(2,1)} %refs_5_.1, ...), custom_call_target="tpu_custom_call" | custom-call | tf_op jit(solution)/shard_map/pallas_call | solution.py:466
  23.7 1.3 %shard_map.182 = (bf16[256,256]{1,0:T(8,128)(2,1)}, bf16[32,256]{1,0:T(8,128)(2,1)}, bf16[4,256]{1,0:T(4,128)(2,1)}, f32[4,256]{1,0:T(4,128)}, f32[4,256]{1,0:T(4,128)}, /*index=5*/f32[3,4]{1,0:T(4,128)}) custom-call(bf16[256,256]{1,0:T(8,128)(2,1)S(1)} %get-tuple-element.10.gx_in, bf16[32,256]{1,0:T(8,128)(2,1)S(1)} %get-tuple-element.11.gbc_in, ...), custom_call_target="tpu_custom_call" | custom-call | tf_op jit(solution)/shard_map/pallas_call | solution.py:500

commit v3 on v2

--- a/solution.py
+++ b/solution.py
@@ -45,7 +45,7 @@
     ssm_ref, cx_ref, cbc_ref, wx_ref, wbc_ref = inputs[9:]
     (
     msg, state, gath, msg_out, state_out, pad_x, pad_bc, dpx, dpbc, dw_ref, taps, raw, back,
-    sem_in, sem_msg, sem_state, sem_gath, sem_taps, sem_back, sem_fin,
+    sem_in, sem_msg, sem_state, sem_gath, sem_taps, sem_back, sem_wx, sem_heads, sem_fin,
     ) = refs
     mine = lax.axis_index("exch")
     me = lax.axis_index("dp")
@@ -102,9 +102,7 @@
                 small[k] = small[k] + tails[k][p : p + 1] * weight
             flag = flag + weight
             big = big + ssm_ref[p].astype(F32) * weight
-        for k in range(depth):
-            msg_dst[k : k + 1] = small[k]
-        msg_dst[depth : depth + 1] = flag
+        msg_dst[...] = jnp.concatenate(small + [flag], axis=0).astype(BF16)
         state_dst[...] = big.astype(BF16)
 
     for offset in range(1, peers):
@@ -214,17 +212,18 @@
 
     for copy in msg_copies:
         copy.wait_recv()
+    got = [msg[z].astype(F32) for z in range(peers)]
     weights = [[None] * peers for _ in range(prompts)]
     seen = jnp.zeros((1, channels + pair), F32)
     for z in range(peers):
-        present = msg[z, depth : depth + 1]
+        present = got[z][depth : depth + 1]
         for j in range(prompts):
             weights[j][z] = jnp.where(seen == float(j), present, 0.0)
         seen = seen + present
     for r in range(responses):
         prev = jnp.zeros((depth, channels + pair), F32)
         for z in range(peers):
-            prev = prev + msg[z, 0:depth] * weights[r // GROUP][z]
+            prev = prev + got[z][0:depth] * weights[r // GROUP][z]
         pad_x[r, base:8] = prev[:, :channels]
         pad_bc[r, base:8] = prev[:, channels:]
 
@@ -303,6 +302,14 @@
         b_grads.append(three(nn, split(score_grad), proj_c))
         c_grads.append(three(nn, split(score_grad.T), proj_b))
 
+    def send_rows(row, sem):
+        part = fin.at[mine, pl.ds(row, 8)]
+        return [remote(part, part, sem, o, along(o)) for o in range(1, peers)]
+
+    fin[mine] = jnp.zeros(fin.shape[1:], F32)
+    fin[mine, 0:taps_n, 0:channels] = grad_wx
+    fin_copies = send_rows(0, sem_wx)
+
     for copy in state_copies:
         copy.wait_recv()
     starts = []
@@ -372,9 +379,8 @@
         bias_grad,
         jnp.where(column == 1, decay_grad, jnp.where(column == 2, skip_grad, 0.0)),
     )
-    fin[mine] = jnp.zeros(fin.shape[1:], F32)
-    fin[mine, 0:taps_n, 0:channels] = grad_wx
     fin[mine, 8 : 8 + heads, 0:half] = head_block
+    fin_copies = fin_copies + send_rows(8, sem_heads)
 
     for copy in taps_copies:
         copy.wait_recv()
@@ -383,9 +389,7 @@
         for d in range(1, DEV_GROUP):
             total = total + taps[q * DEV_GROUP + d, 0:taps_n]
         fin[mine, 16 : 16 + taps_n, q * pair : (q + 1) * pair] = total
-    fin_copies = [
-        remote(fin.at[mine], fin.at[mine], sem_fin, o, along(o)) for o in range(1, peers)
-    ]
+    fin_copies = fin_copies + send_rows(16, sem_fin)
 
     for copy in back_copies:
         copy.wait_recv()
@@ -471,10 +475,10 @@
         scratch_shapes=[pltpu.SMEM(a.shape, a.dtype) for a in args[:5]]
         + [pltpu.VMEM(a.shape, a.dtype) for a in args[5:]]
         + [
-            pltpu.VMEM((peers, 8, channels + pair), F32),
+            pltpu.VMEM((peers, depth + 1, channels + pair), BF16),
             pltpu.VMEM((peers, heads * width, nstate), BF16),
             pltpu.VMEM((slices, rows, pair), BF16),
-            pltpu.VMEM((peers, 8, channels + pair), F32),
+            pltpu.VMEM((peers, depth + 1, channels + pair), BF16),
             pltpu.VMEM((peers, heads * width, nstate), BF16),
             pltpu.VMEM((responses, length + 8, channels), F32),
             pltpu.VMEM((responses, length + 8, pair), F32),
@@ -491,6 +495,8 @@
             dma((2, slices)),
             dma((2, slices)),
             dma((2, peers)),
+            dma((2, peers)),
+            dma((2, peers)),
         ],
         compiler_params=pltpu.CompilerParams(
             collective_id=0, has_side_effects=True

time: 25.1 us -> 23.4 us (0.932)
  Pallas kernels: 24.3 us -> 22.6 us
    pallas_call x1, Pallas kernels: 23.1 us -> 21.3 us  [local(): pl.pallas_call(functools.partial(kernel, peers, slices, groups), out_shap...]
where the time goes in v3:
time: 23.4 us; the launch traced here: 23.3 us
  Pallas kernels  22.6 us (97%)
  between operations  0.65 us (3%)
    pallas_call x1, Pallas kernels, local(): pl.pallas_call(functools.partial(kernel, peers, slices, groups), out_shap...  21.3 us
    pallas_call x1, Pallas kernels, local(): pl.pallas_call(finish, out_shape=outs, in_specs=[vmem] * 4, out_specs=[an...  1.29 us

profile of v3, /device:TPU:0, one launch (start us, length us, event | category | flops | bytes accessed | tf_op | source)
XLA Modules:
  0.0 23.3 jit_solution(3392792940267017481)
XLA Ops:
  0.6 21.3 %shard_map.181 = (bf16[256,256]{1,0:T(8,128)(2,1)S(1)}, bf16[32,256]{1,0:T(8,128)(2,1)S(1)}, bf16[4,256]{1,0:T(4,128)(2,1)S(1)}, f32[4,24,256]{2,1,0:T(8,128)S(1)}) custom-call(s32[2]{0:T(128)} %refs_0_.1, s32[2]{0:T(128)} %refs_1_.1, f32[4]{0:T(128)} %refs_2_.1, f32[4]{0:T(128)} %refs_3_.1, f32[4]{0:T(128)} %refs_4_.1, bf16[256,256]{1,0:T(8,128)(2,1)} %refs_5_.1, ...), custom_call_target="tpu_custom_call" | custom-call | tf_op jit(solution)/shard_map/pallas_call | solution.py:470
  22.0 1.3 %shard_map.182 = (bf16[256,256]{1,0:T(8,128)(2,1)}, bf16[32,256]{1,0:T(8,128)(2,1)}, bf16[4,256]{1,0:T(4,128)(2,1)}, f32[4,256]{1,0:T(4,128)}, f32[4,256]{1,0:T(4,128)}, /*index=5*/f32[3,4]{1,0:T(4,128)}) custom-call(bf16[256,256]{1,0:T(8,128)(2,1)S(1)} %get-tuple-element.10.gx_in, bf16[32,256]{1,0:T(8,128)(2,1)S(1)} %get-tuple-element.11.gbc_in, ...), custom_call_target="tpu_custom_call" | custom-call | tf_op jit(solution)/shard_map/pallas_call | solution.py:506
